TPU v7x, 32 devices: a whole 2x2x4 slice. The times are simulated.
32 devices in a mesh: groups: 2 (over y), row: 4 (over x, core), col: 4 (over z).
Axes of the slice: x: 2, y: 2, z: 4, core: 2. Of those that a mesh axis runs over, the one named last changes fastest.
Arguments:
- inputs: bfloat16 [1536, 4096], P(('groups', 'col'), 'row'), parts along dimension 0, may hold values from -6 to 6
- cotangent: bfloat16 [1536, 4096], P(('groups', 'col'), 'row'), parts along dimension 0, may hold values from -6 to 6
- preactivation: bfloat16 [1536, 8192], P(('groups', 'row'), 'col'), parts along dimension 0, may hold values from -8 to 8
- up_weight: bfloat16 [4096, 8192], P('row', 'col'), may hold values from -0.09375 to 0.09375
- down_weight: bfloat16 [8192, 4096], P('col', 'row'), may hold values from -0.0625 to 0.0625
Outputs:
- grad_input: bfloat16 [1536, 4096], P(('groups', 'col'), 'row'), parts along dimension 0
- grad_up: float32 [8192, 8192], P(('groups', 'row'), 'col'), parts along dimension 0
- grad_down: float32 [16384, 4096], P(('groups', 'col'), 'row'), parts along dimension 0
There are 2 independent parts, one for each index of `groups`. A program takes and returns all parts, laid end to end along the dimension named above; an argument that names none is the same for every part. Nothing has to cross between parts.
All inputs are finite; a program needn't handle non-finite values.
Results may differ from a plain program's by a relative error of at most 0.0049.
Values may be sent and summed in bfloat16 or wider, within the bound.
A program may use at most 128 MiB of HBM per device.

v0:
```python
import math
import jax
import jax.numpy as jnp
from jax import lax
from jax.sharding import PartitionSpec as P


def gelu_pair(values):
    v = values.astype(jnp.float32)
    tanh_arg = 0.7978845608 * (v + 0.044715 * v * v * v)
    tanh_val = jnp.tanh(tanh_arg)
    gelu_value = 0.5 * v * (1.0 + tanh_val)
    gelu_slope = 0.5 * (1.0 + tanh_val) + 0.5 * v * (1.0 - tanh_val * tanh_val) * 0.7978845608 * (
        1.0 + 3.0 * 0.044715 * v * v
    )
    return (gelu_value, gelu_slope)


def per_device(inputs, cotangent, preactivation, up_weight, down_weight):
    inputs_all, cotangent_all = (
        lax.all_gather(inputs, "col", axis=0, tiled=True),
        lax.all_gather(cotangent, "col", axis=0, tiled=True),
    )
    total_tokens = inputs_all.shape[0]
    token_scale = 1.0 / math.sqrt(total_tokens)
    last_dims = (((1,), (1,)), ((), ()))
    first_dims = (((0,), (0,)), ((), ()))
    piece = cotangent_all
    hidden_grad = lax.psum_scatter(
        lax.dot_general(piece, down_weight, last_dims, preferred_element_type=jnp.float32),
        "row",
        scatter_dimension=0,
        tiled=True,
    )
    gelu_value, gelu_slope = gelu_pair(preactivation)
    activation = gelu_value.astype(jnp.bfloat16)
    pre_grad = (hidden_grad * gelu_slope).astype(jnp.bfloat16)
    activation_all, pre_grad_all = (
        lax.all_gather(activation, "row", axis=0, tiled=True),
        lax.all_gather(pre_grad, "row", axis=0, tiled=True),
    )
    piece = pre_grad_all
    grad_input = lax.psum_scatter(
        lax.dot_general(piece, up_weight, last_dims, preferred_element_type=jnp.float32),
        "col",
        scatter_dimension=0,
        tiled=True,
    ).astype(jnp.bfloat16)
    grad_up = (
        lax.dot_general(inputs_all, pre_grad_all, first_dims, preferred_element_type=jnp.float32)
        * token_scale
    )
    grad_down = (
        lax.dot_general(
            activation_all, cotangent_all, first_dims, preferred_element_type=jnp.float32
        )
        * token_scale
    )
    return (grad_input, grad_up, grad_down)


def solution(mesh):
    placed = (
        P(("groups", "col"), "row"),
        P(("groups", "col"), "row"),
        P(("groups", "row"), "col"),
        P("row", "col"),
        P("col", "row"),
    )
    return jax.shard_map(
        per_device,
        mesh=mesh,
        in_specs=placed,
        out_specs=(
            P(("groups", "col"), "row"),
            P(("groups", "row"), "col"),
            P(("groups", "col"), "row"),
        ),
        check_vma=False,
    )
```

profile of v0, /device:TPU:0, one launch (start us, length us, event | category | flops | bytes accessed | tf_op | source)
XLA Modules:
  0.0 287.1 jit_solution(9059382792913873849)
XLA Ops:
  7.2 0.0 all-gather.5.cloned.1.call-start
  7.2 0.7 all-gather.5.cloned.1.call-update
  7.9 0.0 reduce-scatter.3.cloned.1.call-start
  7.9 41.4 %all-gather.5.cloned.1.call-done = bf16[768,1024]{1,0:T(8,128)(2,1)} async-done(((bf16[192,1024]{1,0:T(8,128)(2,1)}), bf16[768,1024]{1,0:T(8,128)(2,1)}) %all-gather.5.cloned.1.call-update) | async-done | bytes 1572880 | tf_op jit(solution)/shard_map/all_gather | solution.py:22
  49.3 8.8 %fusion.11 = f32[768,2048]{1,0:T(8,128)} fusion(bf16[768,1024]{1,0:T(8,128)(2,1)} %all-gather.5.cloned.1.call-done, bf16[2048,1024]{1,0:T(8,128)(2,1)} %param.9), kind=kOutput, calls=%fused_computation.20 | convolution fusion | flops 3221225472 | bytes 12058624 | tf_op jit(solution)/shard_map/dot_general | solution.py:30
  58.1 0.0 copy-start
  58.1 0.0 reduce-scatter.3.cloned.1.call-update
  58.2 0.0 all-gather.7.cloned.1.call-start
  58.2 57.8 %reduce-scatter.3.cloned.1.call-done = f32[192,2048]{1,0:T(8,128)} async-done(((f32[768,2048]{1,0:T(8,128)}), f32[192,2048]{1,0:T(8,128)}) %reduce-scatter.3.cloned.1.call-update) | async-done | bytes 1572880 | tf_op jit(solution)/shard_map/reduce_scatter | solution.py:29
  116.0 0.0 copy-done
  116.0 3.7 %fusion.7 = (bf16[192,2048]{1,0:T(8,128)(2,1)}, bf16[192,2048]{1,0:T(8,128)(2,1)}) fusion(bf16[192,2048]{1,0:T(8,128)(2,1)S(1)} %copy-done, f32[192,2048]{1,0:T(8,128)} %reduce-scatter.3.cloned.1.call-done), kind=kLoop, calls=%fused_computation.16 | loop fusion | flops 8650752 | bytes 3932160 | tf_op jit(solution)/shard_map/convert_element_type | solution.py:36
  119.7 0.0 all-gather.7.cloned.1.call-update
  119.7 0.0 all-gather.9.cloned.1.call-start
  119.8 0.5 all-gather.9.cloned.1.call-update
  120.3 0.0 all-gather.11.cloned.1.call-start
  120.4 0.5 all-gather.11.cloned.1.call-update
  120.9 0.0 reduce-scatter.5.cloned.1.call-start
  121.0 27.4 %all-gather.7.cloned.1.call-done = bf16[768,2048]{1,0:T(8,128)(2,1)} async-done(((bf16[192,2048]{1,0:T(8,128)(2,1)}), bf16[768,2048]{1,0:T(8,128)(2,1)}) %all-gather.7.cloned.1.call-update) | async-done | bytes 3145744 | tf_op jit(solution)/shard_map/all_gather | solution.py:40
  148.4 8.3 %fusion.12 = f32[768,1024]{1,0:T(8,128)} fusion(bf16[768,2048]{1,0:T(8,128)(2,1)} %all-gather.7.cloned.1.call-done, bf16[1024,2048]{1,0:T(8,128)(2,1)} %param.8), kind=kOutput, calls=%fused_computation.21 | convolution fusion | flops 3221225472 | bytes 10485760 | tf_op jit(solution)/shard_map/dot_general | solution.py:44
  156.7 0.0 copy-start.1
  156.7 0.0 reduce-scatter.5.cloned.1.call-update
  156.7 30.2 %all-gather.9.cloned.1.call-done = bf16[768,1024]{1,0:T(8,128)(2,1)} async-done(((bf16[192,1024]{1,0:T(8,128)(2,1)}), bf16[768,1024]{1,0:T(8,128)(2,1)}) %all-gather.9.cloned.1.call-update) | async-done | bytes 1572880 | tf_op jit(solution)/shard_map/all_gather | solution.py:21
  186.9 0.0 copy-done.1
  186.9 7.1 %multiply_bitcast_fusion = f32[1024,2048]{0,1:T(8,128)} fusion(bf16[768,2048]{1,0:T(8,128)(2,1)S(1)} %copy-done.1, bf16[768,1024]{1,0:T(8,128)(2,1)} %all-gather.9.cloned.1.call-done), kind=kOutput, calls=%fused_computation | convolution fusion | flops 3223322624 | bytes 13107200 | tf_op jit(solution)/shard_map/dot_general | solution.py:50
  194.0 0.0 copy-start.2
  194.0 9.4 %copy.8 = f32[1024,2048]{1,0:T(8,128)} copy(f32[1024,2048]{0,1:T(8,128)} %multiply_bitcast_fusion) | data formatting | bytes 16777216
  203.4 12.3 %all-gather.11.cloned.1.call-done = bf16[768,2048]{1,0:T(8,128)(2,1)} async-done(((bf16[192,2048]{1,0:T(8,128)(2,1)}), bf16[768,2048]{1,0:T(8,128)(2,1)}) %all-gather.11.cloned.1.call-update) | async-done | bytes 3145744 | tf_op jit(solution)/shard_map/all_gather | solution.py:39
  215.7 0.0 copy-done.2
  215.7 7.6 %convolution_multiply_fusion = f32[2048,1024]{1,0:T(8,128)} fusion(bf16[768,2048]{1,0:T(8,128)(2,1)} %all-gather.11.cloned.1.call-done, bf16[768,1024]{1,0:T(8,128)(2,1)S(1)} %copy-done.2), kind=kOutput, calls=%fused_computation.1 | convolution fusion | flops 3223322624 | bytes 13107200 | tf_op jit(solution)/shard_map/dot_general | solution.py:54
  223.3 55.0 %reduce-scatter.5.cloned.1.call-done = f32[192,1024]{1,0:T(8,128)} async-done(((f32[768,1024]{1,0:T(8,128)}), f32[192,1024]{1,0:T(8,128)}) %reduce-scatter.5.cloned.1.call-update) | async-done | bytes 786448 | tf_op jit(solution)/shard_map/reduce_scatter | solution.py:43
  278.3 1.9 convert_element_type.14
Async XLA Ops:
  7.2 42.2 %all-gather.5.cloned.1.call-start = ((), (), s32[]{:S(2)}) async-start(), calls=%async_computation.2 | async-start | bytes 1966080 | tf_op jit(solution)/shard_map/all_gather | solution.py:22
  7.9 108.1 %reduce-scatter.3.cloned.1.call-start = ((), (), s32[]{:S(2)}) async-start(), calls=%async_computation.3 | async-start | bytes 7864320 | tf_op jit(solution)/shard_map/reduce_scatter | solution.py:29
  58.1 57.9 %copy-start = (bf16[192,2048]{1,0:T(8,128)(2,1)S(1)}, bf16[192,2048]{1,0:T(8,128)(2,1)}, u32[]{:S(2)}) copy-start(bf16[192,2048]{1,0:T(8,128)(2,1)} %param.7) | copy-start | bytes 2359300
  58.2 90.2 %all-gather.7.cloned.1.call-start = ((), (), s32[]{:S(2)}) async-start(), calls=%async_computation.4 | async-start | bytes 3932160 | tf_op jit(solution)/shard_map/all_gather | solution.py:40
  119.7 67.1 %all-gather.9.cloned.1.call-start = ((), (), s32[]{:S(2)}) async-start(), calls=%async_computation.6 | async-start | bytes 1966080 | tf_op jit(solution)/shard_map/all_gather | solution.py:21
  120.3 95.4 %all-gather.11.cloned.1.call-start = ((), (), s32[]{:S(2)}) async-start(), calls=%async_computation.7 | async-start | bytes 3932160 | tf_op jit(solution)/shard_map/all_gather | solution.py:39
  120.9 157.4 %reduce-scatter.5.cloned.1.call-start = ((), (), s32[]{:S(2)}) async-start(), calls=%async_computation.5 | async-start | bytes 3932160 | tf_op jit(solution)/shard_map/reduce_scatter | solution.py:43
  156.7 30.2 %copy-start.1 = (bf16[768,2048]{1,0:T(8,128)(2,1)S(1)}, bf16[768,2048]{1,0:T(8,128)(2,1)}, u32[]{:S(2)}) copy-start(bf16[768,2048]{1,0:T(8,128)(2,1)} %all-gather.7.cloned.1.call-done) | copy-start | bytes 9437188
  194.0 21.7 %copy-start.2 = (bf16[768,1024]{1,0:T(8,128)(2,1)S(1)}, bf16[768,1024]{1,0:T(8,128)(2,1)}, u32[]{:S(2)}) copy-start(bf16[768,1024]{1,0:T(8,128)(2,1)} %all-gather.5.cloned.1.call-done) | copy-start | bytes 4718596
Sparse Core Ops, SparseCore 0:
  9.5 39.7 all-gather.4
  58.3 57.7 reduce-scatter.2
  119.9 28.4 all-gather.6
  149.8 37.0 all-gather.8
  188.3 27.3 all-gather.10
  217.9 60.3 reduce-scatter.4
where the time goes:
time: 287 us
  waiting for transfers between devices  226 us (79%)
  matrix products  31.8 us (11%)
  between operations  14.1 us (5%)
  local copies, waits for them, and re-layouts  9.45 us (3%)
  other arithmetic  5.61 us (2%)
    reduce_scatter x1, waiting for transfers between devices, per_device(): lax.psum_scatter(lax.dot_general(piece, down_weight, last_dims, preferred...  57.8 us
    reduce_scatter x1, waiting for transfers between devices, per_device(): lax.psum_scatter(lax.dot_general(piece, up_weight, last_dims, preferred_e...  55 us
    all_gather x1, waiting for transfers between devices, per_device(): lax.all_gather(cotangent, 'col', axis=0, tiled=True)  41.4 us
    all_gather x1, waiting for transfers between devices, per_device(): lax.all_gather(inputs, 'col', axis=0, tiled=True)  30.2 us
    all_gather x1, waiting for transfers between devices, per_device(): lax.all_gather(pre_grad, 'row', axis=0, tiled=True)  27.4 us
    all_gather x1, waiting for transfers between devices, per_device(): lax.all_gather(activation, 'row', axis=0, tiled=True)  12.3 us
    unnamed x7, local copies, waits for them, and re-layouts  9.45 us
    dot_general x1, matrix products, per_device(): lax.dot_general(piece, down_weight, last_dims, preferred_element_type=jnp...  8.82 us
  transfers between devices with their start and end apart: 6, of which 6 were waited for; matrix products, arithmetic and copies ran while one was open for 11% of the time, Pallas kernels for 0%

commit v1 on v0

--- a/solution.py
+++ b/solution.py
@@ -3,6 +3,10 @@
 import jax.numpy as jnp
 from jax import lax
 from jax.sharding import PartitionSpec as P
+
+_lift_sides = lambda at_axis, device_axis, x_part: jnp.concatenate(
+    lax.all_to_all(jnp.stack(lax.axis_size(device_axis) * [x_part], 0), device_axis, 0, 0), at_axis
+)
 
 
 def gelu_pair(values):
@@ -37,7 +41,7 @@
     pre_grad = (hidden_grad * gelu_slope).astype(jnp.bfloat16)
     activation_all, pre_grad_all = (
         lax.all_gather(activation, "row", axis=0, tiled=True),
-        lax.all_gather(pre_grad, "row", axis=0, tiled=True),
+        _lift_sides(0, "row", pre_grad),
     )
     piece = pre_grad_all
     grad_input = lax.psum_scatter(

time: 287 us -> 255 us (0.89)
  waiting for transfers between devices: 226 us -> 157 us
  blocking collectives: 0 us -> 39.7 us
  matrix products: 31.8 us -> 28.8 us
    all_to_all x0 -> x1, blocking collectives: none -> 39.7 us  [lax.all_to_all(jnp.stack(lax.axis_size(device_axis) * [x_part], 0), devic...]
    all_gather x1, waiting for transfers between devices: 30.2 us -> 0.02 us  [per_device(): lax.all_gather(inputs, 'col', axis=0, tiled=True)]
    all_gather x1 -> x0, waiting for transfers between devices: 27.4 us -> none  [per_device(): lax.all_gather(pre_grad, 'row', axis=0, tiled=True)]
    all_gather x1, waiting for transfers between devices: 12.3 us -> 2.18 us  [per_device(): lax.all_gather(activation, 'row', axis=0, tiled=True)]
    dot_general x1, matrix products: 8.27 us -> 5.23 us  [per_device(): lax.dot_general(piece, up_weight, last_dims, preferred_element_type=jnp.f...]
  transfers between devices with their start and end apart: 6 -> 5, of which waited for: 6 -> 4; matrix products, arithmetic and copies ran while one was open for 11% -> 13% of each run, Pallas kernels for 0% -> 0%
where the time goes in v1:
time: 255 us
  waiting for transfers between devices  157 us (62%)
  blocking collectives  39.7 us (16%)
  matrix products  28.8 us (11%)
  between operations  13.8 us (5%)
  local copies, waits for them, and re-layouts  9.66 us (4%)
  other arithmetic  5.36 us (2%)
    reduce_scatter x1, waiting for transfers between devices, per_device(): lax.psum_scatter(lax.dot_general(piece, down_weight, last_dims, preferred...  57.1 us
    reduce_scatter x1, waiting for transfers between devices, per_device(): lax.psum_scatter(lax.dot_general(piece, up_weight, last_dims, preferred_e...  55 us
    all_gather x1, waiting for transfers between devices, per_device(): lax.all_gather(cotangent, 'col', axis=0, tiled=True)  41.4 us
    all_to_all x1, blocking collectives, lax.all_to_all(jnp.stack(lax.axis_size(device_axis) * [x_part], 0), devic...  39.7 us
    unnamed x7, local copies, waits for them, and re-layouts  9.28 us
    dot_general x1, matrix products, per_device(): lax.dot_general(piece, down_weight, last_dims, preferred_element_type=jnp...  8.82 us
    dot_general x1, matrix products, per_device(): lax.dot_general(activation_all, cotangent_all, first_dims, preferred_elem...  7.6 us
    dot_general x1, matrix products, per_device(): lax.dot_general(inputs_all, pre_grad_all, first_dims, preferred_element_t...  7.13 us
  transfers between devices with their start and end apart: 5, of which 4 were waited for; matrix products, arithmetic and copies ran while one was open for 13% of the time, Pallas kernels for 0%

profile of v1, /device:TPU:0, one launch (start us, length us, event | category | flops | bytes accessed | tf_op | source)
XLA Modules:
  0.0 254.5 jit_solution(523620881591013865)
XLA Ops:
  7.2 0.0 all-gather.4.cloned.1.call-start
  7.2 0.7 all-gather.4.cloned.1.call-update
  7.9 0.0 reduce-scatter.3.cloned.1.call-start
  7.9 41.4 %all-gather.4.cloned.1.call-done = bf16[768,1024]{1,0:T(8,128)(2,1)} async-done(((bf16[192,1024]{1,0:T(8,128)(2,1)}), bf16[768,1024]{1,0:T(8,128)(2,1)}) %all-gather.4.cloned.1.call-update) | async-done | bytes 1572880 | tf_op jit(solution)/shard_map/all_gather | solution.py:26
  49.3 8.8 %fusion.11 = f32[768,2048]{1,0:T(8,128)} fusion(bf16[768,1024]{1,0:T(8,128)(2,1)} %all-gather.4.cloned.1.call-done, bf16[2048,1024]{1,0:T(8,128)(2,1)} %param.9), kind=kOutput, calls=%fused_computation.20 | convolution fusion | flops 3221225472 | bytes 12058624 | tf_op jit(solution)/shard_map/dot_general | solution.py:34
  58.1 0.0 copy-start
  58.1 0.0 reduce-scatter.3.cloned.1.call-update
  58.2 0.0 all-gather.6.cloned.1.call-start
  58.2 0.7 all-gather.6.cloned.1.call-update
  58.9 0.0 all-gather.8.cloned.1.call-start
  59.0 57.1 %reduce-scatter.3.cloned.1.call-done = f32[192,2048]{1,0:T(8,128)} async-done(((f32[768,2048]{1,0:T(8,128)}), f32[192,2048]{1,0:T(8,128)}) %reduce-scatter.3.cloned.1.call-update) | async-done | bytes 1572880 | tf_op jit(solution)/shard_map/reduce_scatter | solution.py:33
  116.0 0.0 copy-done
  116.0 3.4 %fusion.7 = (bf16[192,2048]{1,0:T(8,128)(2,1)}, bf16[192,2048]{1,0:T(8,128)(2,1)S(1)}) fusion(bf16[192,2048]{1,0:T(8,128)(2,1)S(1)} %copy-done, f32[192,2048]{1,0:T(8,128)} %reduce-scatter.3.cloned.1.call-done), kind=kLoop, calls=%fused_computation.16 | loop fusion | flops 8650752 | bytes 3932160 | tf_op jit(solution)/shard_map/convert_element_type | solution.py:40
  119.5 0.0 all-gather.8.cloned.1.call-update
  119.5 0.0 reduce-scatter.5.cloned.1.call-start
  119.5 0.4 stack.2
  119.9 0.0 copy-start.1
  119.9 39.7 %all_to_all.5 = bf16[4,192,2048]{2,1,0:T(8,128)(2,1)S(1)} all-to-all(bf16[4,192,2048]{2,1,0:T(8,128)(2,1)S(1)} %stack.2), channel_id=1, replica_groups=mesh['groups'=2,'row'=4,'col'=4] {'row'}, dimensions={0} | all-to-all | bytes 6291456 | tf_op jit(solution)/shard_map/all_to_all | solution.py:8
  159.6 0.0 copy-done.1
  159.6 5.2 %fusion.12 = f32[768,1024]{1,0:T(8,128)} fusion(bf16[768,2048]{1,0:T(8,128)(2,1)S(1)} %bitcast.11, bf16[1024,2048]{1,0:T(8,128)(2,1)S(1)} %copy-done.1), kind=kOutput, calls=%fused_computation.21 | convolution fusion | flops 3221225472 | bytes 10485760 | tf_op jit(solution)/shard_map/dot_general | solution.py:48
  164.9 0.0 reduce-scatter.5.cloned.1.call-update
  164.9 0.0 all-gather.6.cloned.1.call-done
  164.9 7.1 %multiply_bitcast_fusion = f32[1024,2048]{0,1:T(8,128)} fusion(bf16[768,2048]{1,0:T(8,128)(2,1)S(1)} %bitcast.12, bf16[768,1024]{1,0:T(8,128)(2,1)} %all-gather.6.cloned.1.call-done), kind=kOutput, calls=%fused_computation | convolution fusion | flops 3223322624 | bytes 13107200 | tf_op jit(solution)/shard_map/dot_general | solution.py:54
  172.0 0.0 copy-start.2
  172.0 9.3 %copy.8 = f32[1024,2048]{1,0:T(8,128)} copy(f32[1024,2048]{0,1:T(8,128)} %multiply_bitcast_fusion) | data formatting | bytes 16777216
  181.3 2.2 all-gather.8.cloned.1.call-done
  183.5 0.0 copy-done.2
  183.5 7.6 %convolution_multiply_fusion = f32[2048,1024]{1,0:T(8,128)} fusion(bf16[768,2048]{1,0:T(8,128)(2,1)} %all-gather.8.cloned.1.call-done, bf16[768,1024]{1,0:T(8,128)(2,1)S(1)} %copy-done.2), kind=kOutput, calls=%fused_computation.1 | convolution fusion | flops 3223322624 | bytes 13107200 | tf_op jit(solution)/shard_map/dot_general | solution.py:58
  191.1 55.0 %reduce-scatter.5.cloned.1.call-done = f32[192,1024]{1,0:T(8,128)} async-done(((f32[768,1024]{1,0:T(8,128)}), f32[192,1024]{1,0:T(8,128)}) %reduce-scatter.5.cloned.1.call-update) | async-done | bytes 786448 | tf_op jit(solution)/shard_map/reduce_scatter | solution.py:47
  246.1 1.9 convert_element_type.14
Async XLA Ops:
  7.2 42.2 %all-gather.4.cloned.1.call-start = ((), (), s32[]{:S(2)}) async-start(), calls=%async_computation.3 | async-start | bytes 1966080 | tf_op jit(solution)/shard_map/all_gather | solution.py:26
  7.9 108.1 %reduce-scatter.3.cloned.1.call-start = ((), (), s32[]{:S(2)}) async-start(), calls=%async_computation.4 | async-start | bytes 7864320 | tf_op jit(solution)/shard_map/reduce_scatter | solution.py:33
  58.1 57.9 %copy-start = (bf16[192,2048]{1,0:T(8,128)(2,1)S(1)}, bf16[192,2048]{1,0:T(8,128)(2,1)}, u32[]{:S(2)}) copy-start(bf16[192,2048]{1,0:T(8,128)(2,1)} %param.7) | copy-start | bytes 2359300
  58.2 106.7 %all-gather.6.cloned.1.call-start = ((), (), s32[]{:S(2)}) async-start(), calls=%async_computation.6 | async-start | bytes 1966080 | tf_op jit(solution)/shard_map/all_gather | solution.py:25
  58.9 124.6 %all-gather.8.cloned.1.call-start = ((), (), s32[]{:S(2)}) async-start(), calls=%async_computation.7 | async-start | bytes 3932160 | tf_op jit(solution)/shard_map/all_gather | solution.py:43
  119.5 126.6 %reduce-scatter.5.cloned.1.call-start = ((), (), s32[]{:S(2)}) async-start(), calls=%async_computation.5 | async-start | bytes 3932160 | tf_op jit(solution)/shard_map/reduce_scatter | solution.py:47
  119.9 39.7 %copy-start.1 = (bf16[1024,2048]{1,0:T(8,128)(2,1)S(1)}, bf16[1024,2048]{1,0:T(8,128)(2,1)}, u32[]{:S(2)}) copy-start(bf16[1024,2048]{1,0:T(8,128)(2,1)} %param.8) | copy-start | bytes 12582916
  172.0 11.5 %copy-start.2 = (bf16[768,1024]{1,0:T(8,128)(2,1)S(1)}, bf16[768,1024]{1,0:T(8,128)(2,1)}, u32[]{:S(2)}) copy-start(bf16[768,1024]{1,0:T(8,128)(2,1)} %all-gather.4.cloned.1.call-done) | copy-start | bytes 4718596
Sparse Core Ops, SparseCore 0:
  9.5 39.7 all-gather.3
  58.3 57.7 reduce-scatter.2
  117.6 37.0 all-gather.5
  156.1 27.3 all-gather.7
  185.6 60.3 reduce-scatter.4
